TPU v7x, 32 devices: a whole 2x2x4 slice. The times are simulated.
32 devices in a mesh: section: 4 (over x, core), dp: 8 (over z, y).
Axes of the slice: x: 2, y: 2, z: 4, core: 2. Of those that a mesh axis runs over, the one named last changes fastest.
Arguments:
- token_ids: int32 [2, 16], P(None, 'dp'), may hold values from 0 to 8191
- target_ids: int32 [2, 16], P(None, 'dp'), may hold values from 0 to 8191
- table: bfloat16 [8192, 4608], P(('section', 'dp')), may hold values from -0.06629126 to 0.06629126
- norm_gain: bfloat16 [2, 4, 4608], P(None, 'section'), may hold values from 0.099609375 to 1.8984375
- w_in: bfloat16 [2, 4, 8, 4608], P(None, 'section'), may hold values from -0.09375 to 0.09375
- w_out: bfloat16 [2, 4, 8, 4608], P(None, 'section'), may hold values from -2 to 2
- final_gain: bfloat16 [4608], replicated, may hold values from 0.099609375 to 1.8984375
Outputs:
- token_loss: float32 [2, 16], P(None, 'dp')
- table_grad: bfloat16 [8192, 4608], P(('section', 'dp'))
All inputs are finite; a program needn't handle non-finite values.
Results may differ from a plain program's by a relative error of at most 0.013.
The roundings to bfloat16 on the way count: a program that leaves them out, or rounds other values in their place, can miss the bound.
Values may be sent and summed in bfloat16 or wider, within the bound.
A program may use at most 64 MiB of HBM per device.

v0:
```python
import math
import jax
import jax.numpy as jnp
from jax import lax
from jax.sharding import PartitionSpec as P

EPS = 1e-06
CAP = 30.0
GELU_C = 0.7978845608028654


def shifted(block, axis, distance):
    devices = range(lax.axis_size(axis))
    route = [((i - distance) % len(devices), i) for i in devices]
    return lax.ppermute(block, axis, route)


def from_root(block, axis, source):
    block = jnp.where(lax.axis_index(axis) == source, block, jnp.zeros_like(block))
    return lax.psum(block, axis)


def gelu_tanh(values):
    return 0.5 * values * (1.0 + jnp.tanh(GELU_C * (values + 0.044715 * values * values * values)))


def gelu_slope(values):
    inner = jnp.tanh(GELU_C * (values + 0.044715 * values * values * values))
    return 0.5 * (1.0 + inner) + 0.5 * values * (1.0 - inner * inner) * GELU_C * (
        1.0 + 3.0 * 0.044715 * values * values
    )


def normalize(rows_in):
    values = rows_in.astype(jnp.float32)
    scale = lax.rsqrt(jnp.mean(values * values, axis=-1, keepdims=True) + EPS)
    return (values * scale, scale)


def norm_back(normed, scale, grad):
    return scale * (grad - normed * jnp.mean(grad * normed, axis=-1, keepdims=True))


def layer_forward(rows_in, gain, first_proj, second_proj):
    normed, scale = normalize(rows_in)
    activated = (normed * gain.astype(jnp.float32)).astype(jnp.bfloat16)
    preact = lax.dot_general(
        activated, first_proj, (((1,), (1,)), ((), ())), preferred_element_type=jnp.float32
    )
    hidden = gelu_tanh(preact).astype(jnp.bfloat16)
    branch = jnp.dot(hidden, second_proj, preferred_element_type=jnp.float32)
    return (rows_in.astype(jnp.float32) + branch).astype(jnp.bfloat16)


def layer_backward(rows_in, gain, first_proj, second_proj, grad_out):
    normed, scale = normalize(rows_in)
    gain_float = gain.astype(jnp.float32)
    activated = (normed * gain_float).astype(jnp.bfloat16)
    preact = lax.dot_general(
        activated, first_proj, (((1,), (1,)), ((), ())), preferred_element_type=jnp.float32
    )
    hidden_grad = lax.dot_general(
        grad_out, second_proj, (((1,), (1,)), ((), ())), preferred_element_type=jnp.float32
    )
    preact_grad = (hidden_grad * gelu_slope(preact)).astype(jnp.bfloat16)
    act_grad = jnp.dot(preact_grad, first_proj, preferred_element_type=jnp.float32)
    return (grad_out.astype(jnp.float32) + norm_back(normed, scale, act_grad * gain_float)).astype(
        jnp.bfloat16
    )


def per_device(token_ids, target_ids, table, norm_gain, w_in, w_out, final_gain):
    sections = lax.axis_size("section")
    section_index = lax.axis_index("section")
    replicas = lax.axis_size("dp")
    replica_index = lax.axis_index("dp")
    batches, width = token_ids.shape
    rows_dev, dim = table.shape
    embed_scale = math.sqrt(dim)
    offset = (section_index * replicas + replica_index) * rows_dev
    columns = jnp.arange(rows_dev, dtype=jnp.int32)
    final_scale = final_gain.astype(jnp.float32)
    ids = lax.all_gather(jnp.concatenate([token_ids, target_ids], 0), "dp", axis=1, tiled=True)
    gains = lax.all_gather(norm_gain, "section", axis=1, tiled=True).reshape(-1, dim)
    first = lax.all_gather(w_in, "section", axis=1, tiled=True).reshape(2 * sections, -1, dim)
    second = lax.all_gather(w_out, "section", axis=1, tiled=True).reshape(2 * sections, -1, dim)
    all_inputs, all_targets = (ids[:batches], ids[batches:])
    wide = all_inputs.shape[1]
    token_count = batches * wide
    chosen = ((all_inputs.reshape(token_count) - offset)[:, None] == columns[None, :]).astype(
        jnp.bfloat16
    )
    looked = jnp.dot(chosen, table, preferred_element_type=jnp.float32).astype(jnp.bfloat16)
    looked = lax.psum(looked, ("section", "dp")).astype(jnp.float32)
    rows = (looked * embed_scale).astype(jnp.bfloat16)

    def forward(rows, weights):
        return (layer_forward(rows, *weights), rows)

    rows, inputs = lax.scan(forward, rows, (gains, first, second))
    normed, scale = normalize(rows)
    head_input = (normed * final_scale).astype(jnp.bfloat16)
    scores = lax.dot_general(
        head_input, table, (((1,), (1,)), ((), ())), preferred_element_type=jnp.float32
    )
    squash = jnp.tanh(scores / CAP)
    capped = CAP * squash
    powers = jnp.exp(capped)
    goal_local = all_targets.reshape(token_count) - offset
    target_mask = goal_local[:, None] == columns[None, :]
    stats = lax.psum(
        jnp.stack(
            [
                jnp.sum(powers, axis=1),
                jnp.sum(jnp.where(target_mask, capped, jnp.float32(0.0)), axis=1),
            ]
        ),
        ("section", "dp"),
    )
    exp_total, target_score = (stats[0], stats[1])
    loss_all = (jnp.log(exp_total) - target_score).reshape(batches, wide)
    token_loss = lax.dynamic_slice_in_dim(loss_all, replica_index * width, width, 1)
    score_grad = (
        (powers / exp_total[:, None] - target_mask.astype(jnp.float32)) * (1.0 - squash * squash)
    ).astype(jnp.bfloat16)
    partial_value = jnp.dot(score_grad, table, preferred_element_type=jnp.float32)
    head_in_grad = lax.psum(partial_value, ("section", "dp"))
    grad = norm_back(normed, scale, head_in_grad * final_scale).astype(jnp.bfloat16)

    def backward(grad, saved):
        return (layer_backward(*saved, grad), None)

    grad, _ = lax.scan(backward, grad, (inputs, gains, first, second), reverse=True)
    head_grad = lax.dot_general(
        score_grad, head_input, (((0,), (0,)), ((), ())), preferred_element_type=jnp.float32
    )
    embed_grad = (
        lax.dot_general(chosen, grad, (((0,), (0,)), ((), ())), preferred_element_type=jnp.float32)
        * embed_scale
    )
    return (token_loss, (head_grad + embed_grad).astype(jnp.bfloat16))


def solution(mesh):
    return jax.shard_map(
        per_device,
        mesh=mesh,
        in_specs=(
            P(None, "dp"),
            P(None, "dp"),
            P(("section", "dp"), None),
            P(None, "section", None),
            P(None, "section", None, None),
            P(None, "section", None, None),
            P(),
        ),
        out_specs=(P(None, "dp"), P(("section", "dp"), None)),
        check_vma=False,
    )
```

profile of v0, /device:TPU:0, one launch (start us, length us, event | category | flops | bytes accessed | tf_op | source)
XLA Modules:
  0.0 419.9 jit_solution(2897440791546498494)
XLA Ops:
  8.2 22.3 %all-gather = s32[8,2,4]{2,1,0:T(2,128)S(1)} all-gather(s32[1,2,4]{2,1,0:T(2,128)S(1)} %bitcast.102), channel_id=1, replica_groups=mesh['section'=4,'dp'=8] {'dp'}, dimensions={0}, use_global_device_ids=true | all-gather | bytes 288 | tf_op jit(solution)/shard_map/all_gather | solution.py:83
  32.1 5.3 %all_gather.13 = bf16[2,4,4608]{2,0,1:T(2,128)(2,1)S(1)} all-gather(bf16[2,1,4608]{2,0,1:T(2,128)(2,1)S(1)} %copy-done.3), channel_id=1, replica_groups=mesh['section'=4,'dp'=8] {'section'}, dimensions={1}, use_global_device_ids=true | all-gather | bytes 92160 | tf_op jit(solution)/shard_map/all_gather | solution.py:84
  38.0 8.2 %all_gather.14 = bf16[2,4,8,4608]{3,2,1,0:T(8,128)(2,1)} all-gather(bf16[2,1,8,4608]{3,2,1,0:T(8,128)(2,1)S(1)} %copy-done.1), channel_id=1, replica_groups=mesh['section'=4,'dp'=8] {'section'}, dimensions={1}, use_global_device_ids=true | all-gather | bytes 737280 | tf_op jit(solution)/shard_map/all_gather | solution.py:85
  46.2 8.1 %all_gather.15 = bf16[2,4,8,4608]{3,2,1,0:T(8,128)(2,1)} all-gather(bf16[2,1,8,4608]{3,2,1,0:T(8,128)(2,1)S(1)} %copy-done.2), channel_id=1, replica_groups=mesh['section'=4,'dp'=8] {'section'}, dimensions={1}, use_global_device_ids=true | all-gather | bytes 737280 | tf_op jit(solution)/shard_map/all_gather | solution.py:86
  54.3 100.7 %all-reduce.3.cloned.1.call-done = bf16[32,4608]{1,0:T(8,128)(2,1)} async-done(((bf16[32,4608]{1,0:T(8,128)(2,1)}), bf16[32,4608]{1,0:T(8,128)(2,1)}) %all-reduce.3.cloned.1.call-update) | async-done | bytes 294928 | tf_op jit(solution)/shard_map/psum | solution.py:94
  156.0 28.2 %while.26 = (s32[]{:T(128)}, bf16[32,4608]{1,0:T(8,128)(2,1)S(1)}, bf16[8,32,4608]{2,1,0:T(8,128)(2,1)}, bf16[8,4608]{1,0:T(8,128)(2,1)}, bf16[8,8,4608]{2,1,0:T...) while((s32[]{:T(128)}, bf16[32,4608]{1,0:T(8,128)(2,1)S(1)}, bf16[8,32,4608]{2,1,0:T(8,128)(2,1)}, ...), condition=%wide.region_3.4_spmd, body=%wide.region_1.3_spmd.sunk | while | flops 6200098 | bytes 2556893 | solution.py:100
  161.5 1.6 fusion.132
  165.0 1.6 fusion.132
  168.5 1.6 fusion.132
  175.6 1.6 fusion.132
  179.1 1.6 fusion.132
  185.4 41.2 %psum.22 = f32[2,32]{1,0:T(2,128)S(1)} all-reduce(f32[2,32]{1,0:T(2,128)S(1)} %pad_maximum_fusion), channel_id=1, replica_groups=mesh['section'=4,'dp'=8] {'section','dp'}, use_global_device_ids=true, to_apply=%region_7.8 | all-reduce | flops 64 | bytes 512 | tf_op jit(solution)/shard_map/psum | solution.py:111
  228.8 3.0 fusion.102
  231.8 123.7 %all-reduce.5.cloned.1.call-done = f32[32,4608]{1,0:T(8,128)} async-done(((f32[32,4608]{1,0:T(8,128)}), f32[32,4608]{1,0:T(8,128)}) %all-reduce.5.cloned.1.call-update) | async-done | bytes 589840 | tf_op jit(solution)/shard_map/psum | solution.py:127
  358.0 50.4 %while.27 = (s32[]{:T(128)}, bf16[32,4608]{1,0:T(8,128)(2,1)S(1)}, bf16[8,32,4608]{2,1,0:T(8,128)(2,1)}, bf16[8,8,4608]{2,1,0:T(8,128)(2,1)}, bf16[8,4608]{1,0:T...) while((s32[]{:T(128)}, bf16[32,4608]{1,0:T(8,128)(2,1)S(1)}, ...), condition=%wide.region_13.14_spmd, body=%wide.region_10.13_spmd.sunk | while | flops 10036515 | bytes 3535725 | solution.py:133
  361.4 1.7 fusion.139
  367.7 1.7 fusion.139
  374.0 1.7 fusion.139
  380.3 1.7 fusion.139
  386.6 1.7 fusion.139
  392.9 1.7 fusion.139
  399.1 1.7 fusion.139
  405.4 1.7 fusion.139
  408.4 4.6 %fusion.91 = bf16[256,4608]{1,0:T(8,128)(2,1)} fusion(f32[256,4608]{1,0:T(8,128)} %fusion.102, bf16[32,4608]{1,0:T(8,128)(2,1)S(1)} %get-tuple-element.159, s32[32]{0:T(128)S(1)} %sub.70), kind=kOutput, calls=%fused_computation.92 | convolution fusion | flops 79044608 | bytes 7372928 | tf_op jit(solution)/shard_map/dot_general | solution.py:138
  (128 shorter events, 66.2 us)
Async XLA Ops:
  7.2 23.5 %copy-start = (bf16[256,4608]{1,0:T(8,128)(2,1)S(1)}, bf16[256,4608]{1,0:T(8,128)(2,1)}, u32[]{:S(2)}) copy-start(bf16[256,4608]{1,0:T(8,128)(2,1)} %param.13) | copy-start | bytes 7077892
  7.2 24.9 %copy-start.4 = (bf16[4608]{0:T(1024)(128)(2,1)S(1)}, bf16[4608]{0:T(1024)(128)(2,1)}, u32[]{:S(2)}) copy-start(bf16[4608]{0:T(1024)(128)(2,1)} %param.17) | copy-start | bytes 27652
  7.2 24.9 %copy-start.3 = (bf16[2,1,4608]{2,0,1:T(2,128)(2,1)S(1)}, bf16[2,1,4608]{2,0,1:T(2,128)(2,1)}, u32[]{:S(2)}) copy-start(bf16[2,1,4608]{2,0,1:T(2,128)(2,1)} %param.14) | copy-start | bytes 55300
  7.2 30.8 %copy-start.1 = (bf16[2,1,8,4608]{3,2,1,0:T(8,128)(2,1)S(1)}, bf16[2,1,8,4608]{3,2,1,0:T(8,128)(2,1)}, u32[]{:S(2)}) copy-start(bf16[2,1,8,4608]{3,2,1,0:T(8,128)(2,1)} %param.15) | copy-start | bytes 442372
  7.2 39.0 %copy-start.2 = (bf16[2,1,8,4608]{3,2,1,0:T(8,128)(2,1)S(1)}, bf16[2,1,8,4608]{3,2,1,0:T(8,128)(2,1)}, u32[]{:S(2)}) copy-start(bf16[2,1,8,4608]{3,2,1,0:T(8,128)(2,1)} %param.16) | copy-start | bytes 442372
  7.2 147.8 %all-reduce.3.cloned.1.call-start = ((), (), s32[]{:S(2)}) async-start(), calls=%async_computation | async-start | bytes 589824 | tf_op jit(solution)/shard_map/psum | solution.py:94
  31.9 323.5 %all-reduce.5.cloned.1.call-start = ((), (), s32[]{:S(2)}) async-start(), calls=%async_computation.1 | async-start | bytes 1179648 | tf_op jit(solution)/shard_map/psum | solution.py:127
Sparse Core Ops, SparseCore 0:
  32.0 122.9 all-reduce.2
  228.3 127.1 all-reduce.4
where the time goes:
time: 422 us; the launch traced here: 420 us
  waiting for transfers between devices  224 us (53%)
  blocking collectives  85 us (20%)
  matrix products  47.9 us (11%)
  other arithmetic  40 us (9%)
  between operations  14.1 us (3%)
  local copies, waits for them, and re-layouts  7.85 us (2%)
    psum x1, waiting for transfers between devices, per_device(): head_in_grad = lax.psum(partial_value, ('section', 'dp'))  124 us
    psum x1, waiting for transfers between devices, per_device(): looked = lax.psum(looked, ('section', 'dp')).astype(jnp.float32)  101 us
    psum x1, blocking collectives, per_device(): lax.psum(jnp.stack([jnp.sum(powers, axis=1), jnp.sum(jnp.where(target_mas...  41.2 us
    all_gather x1, blocking collectives, per_device(): lax.all_gather(jnp.concatenate([token_ids, target_ids], 0), 'dp', axis=1,...  22.3 us
    dot_general x8, matrix products, layer_backward(): jnp.dot(preact_grad, first_proj, preferred_element_type=jnp.float32)  14 us
    dot_general x8, matrix products, layer_forward(): branch = jnp.dot(hidden, second_proj, preferred_element_type=jnp.float32)  12.8 us
    reduce_sum x17, other arithmetic, normalize(): scale = lax.rsqrt(jnp.mean(values * values, axis=-1, keepdims=True) + EPS)  10.7 us
    dot_general x8, matrix products, layer_backward(): lax.dot_general(activated, first_proj, (((1,), (1,)), ((), ())), preferre...  9.88 us
  transfers between devices with their start and end apart: 2, of which 2 were waited for; matrix products, arithmetic and copies ran while one was open for 1% of the time, Pallas kernels for 0%

commit v1 on v0

--- a/solution.py
+++ b/solution.py
@@ -108,14 +108,17 @@
     powers = jnp.exp(capped)
     goal_local = all_targets.reshape(token_count) - offset
     target_mask = goal_local[:, None] == columns[None, :]
-    stats = lax.psum(
-        jnp.stack(
-            [
-                jnp.sum(powers, axis=1),
-                jnp.sum(jnp.where(target_mask, capped, jnp.float32(0.0)), axis=1),
-            ]
+    stats = jnp.sum(
+        lax.all_gather(
+            jnp.stack(
+                [
+                    jnp.sum(powers, axis=1),
+                    jnp.sum(jnp.where(target_mask, capped, jnp.float32(0.0)), axis=1),
+                ]
+            ),
+            ("section", "dp"),
         ),
-        ("section", "dp"),
+        axis=0,
     )
     exp_total, target_score = (stats[0], stats[1])
     loss_all = (jnp.log(exp_total) - target_score).reshape(batches, wide)

time: 422 us -> 445 us (1.055)
  blocking collectives: 85 us -> 111 us
    all_gather x0 -> x1, blocking collectives: none -> 67.1 us  [per_device(): lax.all_gather(jnp.stack([jnp.sum(powers, axis=1), jnp.sum(jnp.where(targ...]
    psum x1 -> x0, blocking collectives: 41.2 us -> none  [per_device(): lax.psum(jnp.stack([jnp.sum(powers, axis=1), jnp.sum(jnp.where(target_mas...]
where the time goes in v1:
time: 445 us; the launch traced here: 442 us
  waiting for transfers between devices  221 us (50%)
  blocking collectives  111 us (25%)
  matrix products  47.9 us (11%)
  other arithmetic  40.1 us (9%)
  between operations  14.1 us (3%)
  local copies, waits for them, and re-layouts  7.85 us (2%)
    psum x1, waiting for transfers between devices, per_device(): head_in_grad = lax.psum(partial_value, ('section', 'dp'))  120 us
    psum x1, waiting for transfers between devices, per_device(): looked = lax.psum(looked, ('section', 'dp')).astype(jnp.float32)  101 us
    all_gather x1, blocking collectives, per_device(): lax.all_gather(jnp.stack([jnp.sum(powers, axis=1), jnp.sum(jnp.where(targ...  67.1 us
    all_gather x1, blocking collectives, per_device(): lax.all_gather(jnp.concatenate([token_ids, target_ids], 0), 'dp', axis=1,...  22.3 us
    dot_general x8, matrix products, layer_backward(): jnp.dot(preact_grad, first_proj, preferred_element_type=jnp.float32)  14 us
    dot_general x8, matrix products, layer_forward(): branch = jnp.dot(hidden, second_proj, preferred_element_type=jnp.float32)  12.8 us
    reduce_sum x17, other arithmetic, normalize(): scale = lax.rsqrt(jnp.mean(values * values, axis=-1, keepdims=True) + EPS)  10.7 us
    dot_general x8, matrix products, layer_backward(): lax.dot_general(activated, first_proj, (((1,), (1,)), ((), ())), preferre...  9.88 us
  transfers between devices with their start and end apart: 2, of which 2 were waited for; matrix products, arithmetic and copies ran while one was open for 1% of the time, Pallas kernels for 0%

profile of v1, /device:TPU:0, one launch (start us, length us, event | category | flops | bytes accessed | tf_op | source)
XLA Modules:
  0.0 442.3 jit_solution(11885547503362035623)
XLA Ops:
  8.2 22.3 %all-gather.1 = s32[8,2,4]{2,1,0:T(2,128)S(1)} all-gather(s32[1,2,4]{2,1,0:T(2,128)S(1)} %bitcast.104), channel_id=1, replica_groups=mesh['section'=4,'dp'=8] {'dp'}, dimensions={0}, use_global_device_ids=true | all-gather | bytes 288 | tf_op jit(solution)/shard_map/all_gather | solution.py:83
  32.1 5.3 %all_gather.19 = bf16[2,4,4608]{2,0,1:T(2,128)(2,1)S(1)} all-gather(bf16[2,1,4608]{2,0,1:T(2,128)(2,1)S(1)} %copy-done.3), channel_id=1, replica_groups=mesh['section'=4,'dp'=8] {'section'}, dimensions={1}, use_global_device_ids=true | all-gather | bytes 92160 | tf_op jit(solution)/shard_map/all_gather | solution.py:84
  38.0 8.2 %all_gather.20 = bf16[2,4,8,4608]{3,2,1,0:T(8,128)(2,1)} all-gather(bf16[2,1,8,4608]{3,2,1,0:T(8,128)(2,1)S(1)} %copy-done.1), channel_id=1, replica_groups=mesh['section'=4,'dp'=8] {'section'}, dimensions={1}, use_global_device_ids=true | all-gather | bytes 737280 | tf_op jit(solution)/shard_map/all_gather | solution.py:85
  46.2 8.1 %all_gather.21 = bf16[2,4,8,4608]{3,2,1,0:T(8,128)(2,1)} all-gather(bf16[2,1,8,4608]{3,2,1,0:T(8,128)(2,1)S(1)} %copy-done.2), channel_id=1, replica_groups=mesh['section'=4,'dp'=8] {'section'}, dimensions={1}, use_global_device_ids=true | all-gather | bytes 737280 | tf_op jit(solution)/shard_map/all_gather | solution.py:86
  54.3 100.7 %all-reduce.3.cloned.1.call-done = bf16[32,4608]{1,0:T(8,128)(2,1)} async-done(((bf16[32,4608]{1,0:T(8,128)(2,1)}), bf16[32,4608]{1,0:T(8,128)(2,1)}) %all-reduce.3.cloned.1.call-update) | async-done | bytes 294928 | tf_op jit(solution)/shard_map/psum | solution.py:94
  156.0 28.2 %while.26 = (s32[]{:T(128)}, bf16[32,4608]{1,0:T(8,128)(2,1)S(1)}, bf16[8,32,4608]{2,1,0:T(8,128)(2,1)}, bf16[8,4608]{1,0:T(8,128)(2,1)}, bf16[8,8,4608]{2,1,0:T...) while((s32[]{:T(128)}, bf16[32,4608]{1,0:T(8,128)(2,1)S(1)}, bf16[8,32,4608]{2,1,0:T(8,128)(2,1)}, ...), condition=%wide.region_3.4_spmd, body=%wide.region_1.3_spmd.sunk | while | flops 6200098 | bytes 2556893 | solution.py:100
  161.5 1.6 fusion.132
  165.0 1.6 fusion.132
  168.5 1.6 fusion.132
  175.6 1.6 fusion.132
  179.1 1.6 fusion.132
  185.4 67.1 %all-gather.2 = f32[32,2,32]{2,1,0:T(2,128)S(1)} all-gather(f32[1,2,32]{2,1,0:T(2,128)S(1)} %maximum_bitcast_fusion), channel_id=2, replica_groups=mesh['section'=4,'dp'=8] {'section','dp'}, dimensions={0}, use_global_device_ids=true | all-gather | bytes 8448 | tf_op jit(solution)/shard_map/all_gather | solution.py:112
  254.8 3.0 fusion.102
  257.8 120.1 %all-reduce.5.cloned.1.call-done = f32[32,4608]{1,0:T(8,128)} async-done(((f32[32,4608]{1,0:T(8,128)}), f32[32,4608]{1,0:T(8,128)}) %all-reduce.5.cloned.1.call-update) | async-done | bytes 589840 | tf_op jit(solution)/shard_map/psum | solution.py:130
  380.5 50.4 %while.27 = (s32[]{:T(128)}, bf16[32,4608]{1,0:T(8,128)(2,1)S(1)}, bf16[8,32,4608]{2,1,0:T(8,128)(2,1)}, bf16[8,8,4608]{2,1,0:T(8,128)(2,1)}, bf16[8,4608]{1,0:T...) while((s32[]{:T(128)}, bf16[32,4608]{1,0:T(8,128)(2,1)S(1)}, ...), condition=%wide.region_13.14_spmd, body=%wide.region_10.13_spmd.sunk | while | flops 10036515 | bytes 3535725 | solution.py:136
  383.8 1.7 fusion.139
  390.1 1.7 fusion.139
  396.4 1.7 fusion.139
  402.7 1.7 fusion.139
  409.0 1.7 fusion.139
  415.3 1.7 fusion.139
  421.6 1.7 fusion.139
  427.9 1.7 fusion.139
  430.8 4.6 %fusion.91 = bf16[256,4608]{1,0:T(8,128)(2,1)} fusion(f32[256,4608]{1,0:T(8,128)} %fusion.102, bf16[32,4608]{1,0:T(8,128)(2,1)S(1)} %get-tuple-element.159, s32[32]{0:T(128)S(1)} %sub.70), kind=kOutput, calls=%fused_computation.92 | convolution fusion | flops 79044608 | bytes 7372928 | tf_op jit(solution)/shard_map/dot_general | solution.py:141
  (129 shorter events, 66.3 us)
Async XLA Ops:
  7.2 23.5 %copy-start = (bf16[256,4608]{1,0:T(8,128)(2,1)S(1)}, bf16[256,4608]{1,0:T(8,128)(2,1)}, u32[]{:S(2)}) copy-start(bf16[256,4608]{1,0:T(8,128)(2,1)} %param.13) | copy-start | bytes 7077892
  7.2 24.9 %copy-start.4 = (bf16[4608]{0:T(1024)(128)(2,1)S(1)}, bf16[4608]{0:T(1024)(128)(2,1)}, u32[]{:S(2)}) copy-start(bf16[4608]{0:T(1024)(128)(2,1)} %param.17) | copy-start | bytes 27652
  7.2 24.9 %copy-start.3 = (bf16[2,1,4608]{2,0,1:T(2,128)(2,1)S(1)}, bf16[2,1,4608]{2,0,1:T(2,128)(2,1)}, u32[]{:S(2)}) copy-start(bf16[2,1,4608]{2,0,1:T(2,128)(2,1)} %param.14) | copy-start | bytes 55300
  7.2 30.8 %copy-start.1 = (bf16[2,1,8,4608]{3,2,1,0:T(8,128)(2,1)S(1)}, bf16[2,1,8,4608]{3,2,1,0:T(8,128)(2,1)}, u32[]{:S(2)}) copy-start(bf16[2,1,8,4608]{3,2,1,0:T(8,128)(2,1)} %param.15) | copy-start | bytes 442372
  7.2 39.0 %copy-start.2 = (bf16[2,1,8,4608]{3,2,1,0:T(8,128)(2,1)S(1)}, bf16[2,1,8,4608]{3,2,1,0:T(8,128)(2,1)}, u32[]{:S(2)}) copy-start(bf16[2,1,8,4608]{3,2,1,0:T(8,128)(2,1)} %param.16) | copy-start | bytes 442372
  7.2 147.8 %all-reduce.3.cloned.1.call-start = ((), (), s32[]{:S(2)}) async-start(), calls=%async_computation | async-start | bytes 589824 | tf_op jit(solution)/shard_map/psum | solution.py:94
  31.9 346.0 %all-reduce.5.cloned.1.call-start = ((), (), s32[]{:S(2)}) async-start(), calls=%async_computation.1 | async-start | bytes 1179648 | tf_op jit(solution)/shard_map/psum | solution.py:130
Sparse Core Ops, SparseCore 0:
  32.0 122.9 all-reduce.2
  254.2 123.6 all-reduce.4
